TPU v7x, 32 devices: a whole 2x2x4 slice. The times are simulated.
32 devices in a mesh: dp: 2 (over y), fsdp: 16 (over z, x, core).
Axes of the slice: x: 2, y: 2, z: 4, core: 2. Of those that a mesh axis runs over, the one named last changes fastest.
Arguments:
- ids: int32 [2, 192], P('dp'), may hold values from 0 to 511
- embed: bfloat16 [512, 8192], P(None, 'fsdp'), may hold values from -32 to 32
- gain: bfloat16 [8192], P('fsdp'), may hold values from 0.099609375 to 1.8984375
- w_in: bfloat16 [3, 4096, 8192], P(None, 'fsdp'), may hold values from -0.0625 to 0.0625
- feat_filter: float32 [3, 256, 7], P(None, 'fsdp'), may hold values from -2.4 to 2.4
- inner_filter: float32 [256, 7], P('fsdp'), may hold values from -2.4 to 2.4
- w_out: bfloat16 [4096, 8192], P(None, 'fsdp'), may hold values from -0.09375 to 0.09375
- cotangent: bfloat16 [2, 192, 8192], P('dp', None, 'fsdp'), may hold values from -6 to 6
- right_prev: bfloat16 [8192, 256], P('fsdp'), may hold values from -6 to 6
Outputs:
- block_out: bfloat16 [2, 192, 8192], P('dp', None, 'fsdp')
- filter_grad: float32 [4, 256, 7], P(None, 'fsdp')
- basis: bfloat16 [4096, 256], P('fsdp')
- right_factor: float32 [8192, 256], P('fsdp')
All inputs are finite; a program needn't handle non-finite values.
Results may differ from a plain program's by a relative error of at most 0.014.
The roundings to bfloat16 on the way count: a program that leaves them out, or rounds other values in their place, can miss the bound.
Values may be sent and summed in bfloat16 or wider, within the bound.
No kernel may reach another device: no remote copies, remote signals or barrier semaphores. Data moves between devices by JAX's collectives and lax.ppermute only.
A program may use at most 128 MiB of HBM per device.

v0:
```python
import jax
import jax.numpy as jnp
from jax import lax
from jax.sharding import PartitionSpec as P

D = 8192
C = 4096
GROUP = 16


def shifted(signal, lag, tap_count):
    padded = jnp.pad(signal, ((tap_count - 1, 0), (0, 0)))
    first = tap_count - 1 - lag
    return padded[first : first + signal.shape[0]]


def causal(signal, tap_table):
    tap_count = tap_table.shape[0]
    result = jnp.zeros(signal.shape, jnp.float32)
    for lag in range(tap_count):
        result = result + tap_table[lag][None, :] * shifted(signal, lag, tap_count)
    return result


def anticausal(signal, tap_table):
    tap_count = tap_table.shape[0]
    padded = jnp.pad(signal, ((0, tap_count - 1), (0, 0)))
    result = jnp.zeros(signal.shape, jnp.float32)
    for lag in range(tap_count):
        result = result + tap_table[lag][None, :] * padded[lag : lag + signal.shape[0]]
    return result


def tap_sums(gradient, signal, tap_count):
    listing = []
    for lag in range(tap_count):
        listing.append(jnp.sum(gradient * shifted(signal, lag, tap_count), axis=0))
    stacked = jnp.stack(listing, axis=0)
    grouped = stacked.reshape(tap_count, stacked.shape[1] // GROUP, GROUP).sum(axis=2)
    return grouped.T


def expand(filters):
    return jnp.repeat(filters.T, GROUP, axis=1)


def per_device(ids, embed, gain, w_in, feat_filter, inner_filter, w_out, cotangent, right_prev):
    tokens = ids[0]
    length = tokens.shape[0]
    tap_count = inner_filter.shape[1]
    onehot = (tokens[:, None] == jnp.arange(embed.shape[0], dtype=jnp.int32)[None, :]).astype(
        jnp.bfloat16
    )
    x_cols = jnp.dot(onehot, embed, preferred_element_type=jnp.float32)
    square_sums = lax.psum(jnp.sum(x_cols * x_cols, axis=1), "fsdp")
    factor = lax.rsqrt(square_sums / D + 1e-05)
    normed_cols = (x_cols * factor[:, None] * gain.astype(jnp.float32)[None, :]).astype(
        jnp.bfloat16
    )
    projected = jnp.einsum(
        "ld,kcd->klc",
        lax.all_gather(normed_cols, "fsdp", axis=1, tiled=True),
        w_in,
        preferred_element_type=jnp.float32,
    )
    rounded = lax.optimization_barrier(projected.astype(jnp.bfloat16)).astype(jnp.float32)
    query, key_in, value = (rounded[0], rounded[1], rounded[2])
    query_conv = causal(query, expand(feat_filter[0]))
    key_conv = causal(key_in, expand(feat_filter[1]))
    value_conv = causal(value, expand(feat_filter[2]))
    gated = key_conv * value_conv
    inner_table = expand(inner_filter)
    window = causal(gated, inner_table)
    gated_out = (query_conv * window).astype(jnp.bfloat16)
    cot_cols = cotangent[0]
    shard_piece = lax.all_gather(gated_out, "fsdp", axis=1, tiled=True)
    weight_rows = w_out
    mixed_sum = jnp.dot(shard_piece, weight_rows, preferred_element_type=jnp.float32)
    term = jnp.einsum("lc,ld->cd", shard_piece, cot_cols, preferred_element_type=jnp.float32)
    mixed_sum, grad_part = (mixed_sum, term)
    block_out = (x_cols + mixed_sum).astype(jnp.bfloat16)[None]
    weight_rows = w_out
    mixed_grad = lax.psum_scatter(
        jnp.einsum("cd,ld->cl", weight_rows, cot_cols, preferred_element_type=jnp.float32),
        "fsdp",
        scatter_dimension=0,
        tiled=True,
    ).T
    query_grad = mixed_grad * window
    window_grad = mixed_grad * query_conv
    gated_grad = anticausal(window_grad, inner_table)
    key_grad = gated_grad * value_conv
    value_grad = gated_grad * key_conv
    norm_factor = 1.0 / jnp.sqrt(jnp.float32(lax.axis_size("dp") * length))
    filter_part = (
        jnp.stack(
            [
                tap_sums(query_grad, query, tap_count),
                tap_sums(key_grad, key_in, tap_count),
                tap_sums(value_grad, value, tap_count),
                tap_sums(window_grad, gated, tap_count),
            ],
            axis=0,
        )
        * norm_factor
    )
    grad_total, filter_grad = (
        lax.psum(grad_part.astype(jnp.bfloat16), "dp").astype(jnp.float32),
        lax.psum(filter_part.astype(jnp.bfloat16), "dp").astype(jnp.float32),
    )
    grad_half = grad_total.astype(jnp.bfloat16)
    grad_rows_own = lax.all_to_all(grad_half, "fsdp", split_axis=0, concat_axis=1, tiled=True)
    panel_own = jnp.dot(
        grad_rows_own,
        lax.all_gather(right_prev, "fsdp", axis=0, tiled=True),
        preferred_element_type=jnp.float32,
    ).astype(jnp.bfloat16)
    root_scale = jnp.sqrt(jnp.float32(C))
    gram_local = jnp.einsum("cr,cs->rs", panel_own, panel_own, preferred_element_type=jnp.float32)
    gram_matrix = lax.psum(gram_local, "fsdp")
    lower_factor = jnp.linalg.cholesky(gram_matrix)
    solved = jax.scipy.linalg.solve_triangular(
        lower_factor, panel_own.astype(jnp.float32).T, lower=True
    ).T
    basis_own = (solved * root_scale).astype(jnp.bfloat16)
    right_raw = jnp.einsum(
        "cd,cr->dr",
        grad_half,
        lax.all_gather(basis_own, "fsdp", axis=0, tiled=True),
        preferred_element_type=jnp.float32,
    )
    column_sums = lax.psum(jnp.sum(right_raw * right_raw, axis=0), "fsdp")
    right_factor = right_raw * lax.rsqrt(column_sums / D + 1e-06)[None, :]
    return (block_out, filter_grad, basis_own, right_factor)


def solution(mesh):
    placed = (
        P("dp", None),
        P(None, "fsdp"),
        P("fsdp"),
        P(None, "fsdp", None),
        P(None, "fsdp", None),
        P("fsdp", None),
        P(None, "fsdp"),
        P("dp", None, "fsdp"),
        P("fsdp", None),
    )
    return jax.shard_map(
        per_device,
        mesh=mesh,
        in_specs=placed,
        out_specs=(P("dp", None, "fsdp"), P(None, "fsdp", None), P("fsdp", None), P("fsdp", None)),
        check_vma=False,
    )
```

profile of v0, /device:TPU:0, one launch (start us, length us, event | category | flops | bytes accessed | tf_op | source)
XLA Modules:
  0.0 699.4 jit_solution(17935779332028869934)
XLA Ops:
  7.2 0.7 convert_element_type.108
  8.2 1.1 multiply_reduce_fusion.1
  9.3 34.9 %psum.35 = f32[192]{0:T(256)S(1)} all-reduce(f32[192]{0:T(256)S(1)} %get-tuple-element.121), channel_id=1, replica_groups=mesh['dp'=2,'fsdp'=16] {'fsdp'}, use_global_device_ids=true, to_apply=%region_1.0 | all-reduce | flops 192 | bytes 1536 | tf_op jit(solution)/shard_map/psum | solution.py:55
  44.2 0.8 multiply_convert_fusion
  45.1 5.4 fusion.14
  55.0 34.7 %all-gather.5.cloned.1.call-done = bf16[192,8192]{1,0:T(8,128)(2,1)} async-done(((bf16[192,512]{1,0:T(8,128)(2,1)}), bf16[192,8192]{1,0:T(8,128)(2,1)}) %all-gather.5.cloned.1.call-update) | async-done | bytes 3145744 | tf_op jit(solution)/shard_map/all_gather | solution.py:62
  89.7 9.8 %fusion.6 = bf16[3,192,256]{2,1,0:T(8,128)(2,1)S(1)} fusion(bf16[3,256,8192]{2,1,0:T(8,128)(2,1)} %param.12, bf16[192,8192]{1,0:T(8,128)(2,1)} %all-gather.5.cloned.1.call-done), kind=kOutput, calls=%fused_computation.8 | convolution fusion | flops 2416066560 | bytes 16023552 | tf_op jit(solution)/shard_map/ld,kcd->klc/dot_general | solution.py:60
  99.6 58.3 %reduce-scatter.2.cloned.1.call-done = f32[256,192]{0,1:T(8,128)} async-done(((f32[4096,192]{0,1:T(8,128)}), f32[256,192]{0,1:T(8,128)}) %reduce-scatter.2.cloned.1.call-update) | async-done | bytes 196624 | tf_op jit(solution)/shard_map/reduce_scatter | solution.py:83
  158.0 1.1 bitcast_multiply_fusion
  159.1 1.0 fusion.28
  160.1 0.8 fusion.29
  161.0 2.6 multiply_reduce_fusion.23
  164.3 38.0 %all-gather.7.cloned.1.call-done = bf16[192,4096]{1,0:T(8,128)(2,1)} async-done(((bf16[192,256]{1,0:T(8,128)(2,1)}), bf16[192,4096]{1,0:T(8,128)(2,1)}) %all-gather.7.cloned.1.call-update) | async-done | bytes 1572880 | tf_op jit(solution)/shard_map/all_gather | solution.py:76
  202.3 4.7 convolution_convert_fusion
  207.7 106.5 %all-reduce.9.cloned.1.call-done = bf16[4096,512]{1,0:T(8,128)(2,1)} async-done(((bf16[4096,512]{1,0:T(8,128)(2,1)}), bf16[4096,512]{1,0:T(8,128)(2,1)}) %all-reduce.9.cloned.1.call-update) | async-done | bytes 4194320 | tf_op jit(solution)/shard_map/psum | solution.py:108
  314.2 6.4 copy.22
  320.6 5.7 all-to-all-start
  326.3 94.7 %all-gather.9.cloned.1.call-done = bf16[8192,256]{1,0:T(8,128)(2,1)} async-done(((bf16[512,256]{1,0:T(8,128)(2,1)}), bf16[8192,256]{1,0:T(8,128)(2,1)}) %all-gather.9.cloned.1.call-update) | async-done | bytes 4194320 | tf_op jit(solution)/shard_map/all_gather | solution.py:115
  421.0 6.5 all-to-all-done
  427.4 4.8 convolution_convert_fusion.1
  432.2 0.9 fusion.31
  434.0 103.0 %all-reduce.11.cloned.1.call-done = f32[256,256]{0,1:T(8,128)} async-done(((f32[256,256]{0,1:T(8,128)}), f32[256,256]{0,1:T(8,128)}) %all-reduce.11.cloned.1.call-update) | async-done | bytes 262160 | tf_op jit(solution)/shard_map/psum | solution.py:120
  537.0 1.8 copy.24
  538.8 1.1 fusion.12
  540.6 11.7 %cholesky.50 = f32[128,128]{1,0:T(8,128)S(1)} custom-call(f32[128,128]{1,0:T(8,128)S(1)} %cholesky.118), custom_call_target="Cholesky" | custom-call | tf_op jit(solution)/shard_map/jit(cholesky)/cholesky | solution.py:121
  553.6 9.8 %custom-call.15 = f32[1,128,128]{1,2,0:T(8,128)S(1)} custom-call(f32[1,128,128]{2,1,0:T(8,128)S(1)} %get-tuple-element.89), custom_call_target="InvertDiagBlocksLowerTriangular" | custom-call | tf_op jit(solution)/shard_map/jit(cholesky)/cholesky | solution.py:121
  563.4 1.7 constant_dynamic-update-slice_fusion.29
  565.1 1.1 convolution_subtract_fusion.1
  566.2 11.7 %cholesky.105 = f32[128,128]{1,0:T(8,128)S(1)} custom-call(f32[128,128]{1,0:T(8,128)S(1)} %convolution_subtract_fusion.1), custom_call_target="Cholesky" | custom-call | tf_op jit(solution)/shard_map/jit(cholesky)/cholesky | solution.py:121
  577.9 1.3 compare_reduce_fusion.1
  581.7 1.7 select_select_fusion
  583.4 0.7 triangular_solve.59
  584.2 6.8 while.1
  584.8 2.9 bitcast_dynamic-update-slice_fusion.2
  588.2 2.8 bitcast_dynamic-update-slice_fusion.2
  591.0 20.5 %custom-call.16 = f32[2,128,128]{1,2,0:T(8,128)S(1)} custom-call(f32[2,128,128]{2,1,0:T(8,128)} %get-tuple-element.11), custom_call_target="InvertDiagBlocksLowerTriangular" | custom-call | tf_op jit(solution)/shard_map/jit(_solve_triangular)/triangular_solve | solution.py:122
  611.8 1.2 convolution_subtract_fusion
  614.0 1.9 multiply_reduce_fusion.2
  616.6 2.0 multiply_reduce_fusion.29
  620.1 0.8 stack.112
  620.9 0.8 stack.113
  622.1 5.0 psum.36
  627.8 3.8 fusion.9
  631.6 0.8 copy.27
  632.4 23.5 %all-gather.11.cloned.1.call-done = bf16[4096,256]{0,1:T(8,128)(2,1)} async-done(((bf16[256,256]{0,1:T(8,128)(2,1)}), bf16[4096,256]{0,1:T(8,128)(2,1)}) %all-gather.11.cloned.1.call-update) | async-done | bytes 2097168 | tf_op jit(solution)/shard_map/all_gather | solution.py:129
  655.9 4.2 multiply_reduce_fusion
  660.1 31.6 %psum.39 = f32[256]{0:T(256)S(1)} all-reduce(f32[256]{0:T(256)S(1)} %get-tuple-element.125), channel_id=1, replica_groups=mesh['dp'=2,'fsdp'=16] {'fsdp'}, use_global_device_ids=true, to_apply=%region_43.44 | all-reduce | flops 256 | bytes 2048 | tf_op jit(solution)/shard_map/psum | solution.py:132
  691.7 0.8 broadcast_multiply_fusion
  (174 shorter events, 16.0 us)
Async XLA Ops:
  7.2 1.1 copy-start
  7.2 82.5 %all-gather.5.cloned.1.call-start = ((), (), s32[]{:S(2)}) async-start(), calls=%async_computation.2 | async-start | bytes 3342336 | tf_op jit(solution)/shard_map/all_gather | solution.py:62
  45.0 5.5 copy-start.8
  45.0 6.6 copy-start.9
  45.1 112.9 %reduce-scatter.2.cloned.1.call-start = ((), (), s32[]{:S(2)}) async-start(), calls=%async_computation.4 | async-start | bytes 3342336 | tf_op jit(solution)/shard_map/reduce_scatter | solution.py:83
  50.5 151.8 %all-gather.7.cloned.1.call-start = ((), (), s32[]{:S(2)}) async-start(), calls=%async_computation.3 | async-start | bytes 1671168 | tf_op jit(solution)/shard_map/all_gather | solution.py:76
  99.5 102.8 %copy-start.7 = (bf16[1,192,512]{2,1,0:T(8,128)(2,1)S(1)}, bf16[1,192,512]{2,1,0:T(8,128)(2,1)}, u32[]{:S(2)}) copy-start(bf16[1,192,512]{2,1,0:T(8,128)(2,1)} %param.16) | copy-start | bytes 589828
  99.6 61.3 %copy-start.3 = (f32[192,256]{1,0:T(8,128)}, f32[192,256]{1,0:T(8,128)S(1)}, u32[]{:S(2)}) copy-start(f32[192,256]{1,0:T(8,128)S(1)} %get-tuple-element.84) | copy-start | bytes 589828
  159.1 48.0 %copy-start.4 = (f32[192,256]{1,0:T(8,128)}, f32[192,256]{1,0:T(8,128)S(1)}, u32[]{:S(2)}) copy-start(f32[192,256]{1,0:T(8,128)S(1)} %get-tuple-element.79) | copy-start | bytes 589828
  161.0 46.1 %copy-start.2 = (f32[192,256]{1,0:T(8,128)}, f32[192,256]{1,0:T(8,128)S(1)}, u32[]{:S(2)}) copy-start(f32[192,256]{1,0:T(8,128)S(1)} %mul.459) | copy-start | bytes 589828
  164.2 150.0 %all-reduce.9.cloned.1.call-start = ((), (), s32[]{:S(2)}) async-start(), calls=%async_computation.5 | async-start | bytes 8388608 | tf_op jit(solution)/shard_map/psum | solution.py:108
  207.1 213.9 %all-gather.9.cloned.1.call-start = ((), (), s32[]{:S(2)}) async-start(), calls=%async_computation.6 | async-start | bytes 4456448 | tf_op jit(solution)/shard_map/all_gather | solution.py:115
  320.6 106.8 %all-to-all-start = ((bf16[16,256,512]{1,2,0:T(8,128)(2,1)}), bf16[16,256,512]{1,2,0:T(8,128)(2,1)}, u32[]{:S(2)}, u32[]{:S(2)}) async-start(bf16[16,256,512]{1,2,0:T(8,128)(2,1)} %copy.22), calls=%async_computation.1 | async-start | bytes 8388608 | tf_op jit(solution)/shard_map/all_to_all | solution.py:112
  326.2 210.8 %all-reduce.11.cloned.1.call-start = ((), (), s32[]{:S(2)}) async-start(), calls=%async_computation.7 | async-start | bytes 524288 | tf_op jit(solution)/shard_map/psum | solution.py:120
  433.2 222.7 %all-gather.11.cloned.1.call-start = ((), (), s32[]{:S(2)}) async-start(), calls=%async_computation.8 | async-start | bytes 2228224 | tf_op jit(solution)/shard_map/all_gather | solution.py:129
  434.0 193.8 %copy-start.1 = (bf16[192,4096]{1,0:T(8,128)(2,1)S(1)}, bf16[192,4096]{1,0:T(8,128)(2,1)}, u32[]{:S(2)}) copy-start(bf16[192,4096]{1,0:T(8,128)(2,1)} %all-gather.7.cloned.1.call-done) | copy-start | bytes 4718596
  539.9 0.7 copy-start.6
  616.6 15.0 %copy-start.5 = (bf16[256,256]{0,1:T(8,128)(2,1)S(1)}, bf16[256,256]{0,1:T(8,128)(2,1)}, u32[]{:S(2)}) copy-start(bf16[256,256]{0,1:T(8,128)(2,1)} %fusion.19) | copy-start | bytes 393220
Sparse Core Ops, SparseCore 0:
  45.2 44.4 all-gather.4
  93.5 64.4 reduce-scatter.1
  164.4 37.9 all-gather.6
  207.2 106.9 all-reduce.8
  316.4 104.4 all-gather.8
  433.3 103.7 all-reduce.10
  614.1 41.7 all-gather.10
where the time goes:
time: 700 us; the launch traced here: 699 us
  waiting for transfers between devices  466 us (67%)
  other arithmetic  73.8 us (11%)
  blocking collectives  71.5 us (10%)
  matrix products  39.3 us (6%)
  local copies, waits for them, and re-layouts  26.9 us (4%)
  between operations  15.8 us (2%)
    psum x1, waiting for transfers between devices, per_device(): lax.psum(grad_part.astype(jnp.bfloat16), 'dp').astype(jnp.float32)  107 us
    psum x1, waiting for transfers between devices, per_device(): gram_matrix = lax.psum(gram_local, 'fsdp')  103 us
    all_gather x1, waiting for transfers between devices, per_device(): lax.all_gather(right_prev, 'fsdp', axis=0, tiled=True)  94.7 us
    reduce_scatter x1, waiting for transfers between devices, per_device(): lax.psum_scatter(jnp.einsum('cd,ld->cl', weight_rows, cot_cols, preferred...  58.3 us
    all_gather x1, waiting for transfers between devices, per_device(): shard_piece = lax.all_gather(gated_out, 'fsdp', axis=1, tiled=True)  38 us
    another operation x7, other arithmetic, per_device(): lower_factor = jnp.linalg.cholesky(gram_matrix)  36.4 us
    psum x1, blocking collectives, per_device(): square_sums = lax.psum(jnp.sum(x_cols * x_cols, axis=1), 'fsdp')  34.9 us
    all_gather x1, waiting for transfers between devices, per_device(): lax.all_gather(normed_cols, 'fsdp', axis=1, tiled=True)  34.7 us
  transfers between devices with their start and end apart: 8, of which 8 were waited for; matrix products, arithmetic and copies ran while one was open for 6% of the time, Pallas kernels for 0%

commit v1 on v0

--- a/solution.py
+++ b/solution.py
@@ -73,7 +73,12 @@
     window = causal(gated, inner_table)
     gated_out = (query_conv * window).astype(jnp.bfloat16)
     cot_cols = cotangent[0]
-    shard_piece = lax.all_gather(gated_out, "fsdp", axis=1, tiled=True)
+    ring = [gated_out]
+    for hop in range(15):
+        ring.append(lax.ppermute(ring[-1], "fsdp", [(dev, (dev + 1) % 16) for dev in range(16)]))
+    shard_piece = jnp.roll(
+        jnp.concatenate(ring[::-1], axis=1), (lax.axis_index("fsdp") + 1) * ring[0].shape[1], axis=1
+    )
     weight_rows = w_out
     mixed_sum = jnp.dot(shard_piece, weight_rows, preferred_element_type=jnp.float32)
     term = jnp.einsum("lc,ld->cd", shard_piece, cot_cols, preferred_element_type=jnp.float32)

time: 700 us -> 760 us (1.086)
  waiting for transfers between devices: 466 us -> 530 us
  other arithmetic: 73.8 us -> 64.6 us
  local copies, waits for them, and re-layouts: 26.9 us -> 35.2 us
    ppermute x0 -> x15, waiting for transfers between devices: none -> 101 us  [per_device(): lax.ppermute(ring[-1], 'fsdp', [(dev, (dev + 1) % 16) for dev in range(16)])]
    all_gather x1 -> x0, waiting for transfers between devices: 38 us -> none  [per_device(): shard_piece = lax.all_gather(gated_out, 'fsdp', axis=1, tiled=True)]
    unnamed x46 -> x95, local copies, waits for them, and re-layouts: 2.47 us -> 15.9 us
  transfers between devices with their start and end apart: 8 -> 22, of which waited for: 8 -> 22; matrix products, arithmetic and copies ran while one was open for 6% -> 5% of each run, Pallas kernels for 0% -> 0%
where the time goes in v1:
time: 760 us; the launch traced here: 759 us
  waiting for transfers between devices  530 us (70%)
  blocking collectives  71.5 us (9%)
  other arithmetic  64.6 us (8%)
  matrix products  35.3 us (5%)
  local copies, waits for them, and re-layouts  35.2 us (5%)
  between operations  16.1 us (2%)
    psum x1, waiting for transfers between devices, per_device(): lax.psum(grad_part.astype(jnp.bfloat16), 'dp').astype(jnp.float32)  105 us
    psum x1, waiting for transfers between devices, per_device(): gram_matrix = lax.psum(gram_local, 'fsdp')  104 us
    ppermute x15, waiting for transfers between devices, per_device(): lax.ppermute(ring[-1], 'fsdp', [(dev, (dev + 1) % 16) for dev in range(16)])  101 us
    all_gather x1, waiting for transfers between devices, per_device(): lax.all_gather(right_prev, 'fsdp', axis=0, tiled=True)  94.5 us
    reduce_scatter x1, waiting for transfers between devices, per_device(): lax.psum_scatter(jnp.einsum('cd,ld->cl', weight_rows, cot_cols, preferred...  58.4 us
    psum x1, blocking collectives, per_device(): square_sums = lax.psum(jnp.sum(x_cols * x_cols, axis=1), 'fsdp')  34.9 us
    another operation x7, other arithmetic, per_device(): lower_factor = jnp.linalg.cholesky(gram_matrix)  34.6 us
    all_gather x1, waiting for transfers between devices, per_device(): lax.all_gather(normed_cols, 'fsdp', axis=1, tiled=True)  34.1 us
  transfers between devices with their start and end apart: 22, of which 22 were waited for; matrix products, arithmetic and copies ran while one was open for 5% of the time, Pallas kernels for 0%

profile of v1, /device:TPU:0, one launch (start us, length us, event | category | flops | bytes accessed | tf_op | source)
XLA Modules:
  0.0 759.4 jit_solution(17949368555458908828)
XLA Ops:
  8.2 1.1 multiply_reduce_fusion.1
  9.3 34.9 %psum.35 = f32[192]{0:T(256)S(1)} all-reduce(f32[192]{0:T(256)S(1)} %get-tuple-element.121), channel_id=1, replica_groups=mesh['dp'=2,'fsdp'=16] {'fsdp'}, use_global_device_ids=true, to_apply=%region_1.0 | all-reduce | flops 192 | bytes 1536 | tf_op jit(solution)/shard_map/psum | solution.py:55
  45.1 5.4 fusion.24
  55.6 34.1 %all-gather.4.cloned.1.call-done = bf16[192,8192]{1,0:T(8,128)(2,1)} async-done(((bf16[192,512]{1,0:T(8,128)(2,1)}), bf16[192,8192]{1,0:T(8,128)(2,1)}) %all-gather.4.cloned.1.call-update) | async-done | bytes 3145744 | tf_op jit(solution)/shard_map/all_gather | solution.py:62
  89.7 9.8 %fusion.14 = bf16[3,192,256]{2,1,0:T(8,128)(2,1)S(1)} fusion(bf16[3,256,8192]{2,1,0:T(8,128)(2,1)} %param.12, bf16[192,8192]{1,0:T(8,128)(2,1)} %all-gather.4.cloned.1.call-done), kind=kOutput, calls=%fused_computation.11 | convolution fusion | flops 2416066560 | bytes 16023552 | tf_op jit(solution)/shard_map/ld,kcd->klc/dot_general | solution.py:60
  99.6 58.4 %reduce-scatter.2.cloned.1.call-done = f32[256,192]{0,1:T(8,128)} async-done(((f32[4096,192]{0,1:T(8,128)}), f32[256,192]{0,1:T(8,128)}) %reduce-scatter.2.cloned.1.call-update) | async-done | bytes 196624 | tf_op jit(solution)/shard_map/reduce_scatter | solution.py:88
  157.9 1.2 bitcast_multiply_fusion
  159.1 1.0 fusion.40
  160.4 1.0 multiply_reduce_fusion.23
  161.5 6.7 collective-permute-done
  168.2 6.7 collective-permute-done.1
  174.9 6.7 collective-permute-done.2
  181.7 6.7 collective-permute-done.3
  188.4 6.7 collective-permute-done.4
  195.1 6.7 collective-permute-done.5
  201.9 6.7 collective-permute-done.6
  208.6 6.7 collective-permute-done.7
  215.4 6.7 collective-permute-done.8
  222.1 6.7 collective-permute-done.9
  229.5 6.7 collective-permute-done.10
  236.9 6.7 collective-permute-done.11
  244.3 6.7 collective-permute-done.12
  251.6 6.8 collective-permute-done.13
  258.6 7.0 collective-permute-done.14
  275.0 1.7 copy-done.1
  276.7 3.3 convolution_convert_fusion
  280.6 104.7 %all-reduce.9.cloned.1.call-done = bf16[4096,512]{1,0:T(8,128)(2,1)} async-done(((bf16[4096,512]{1,0:T(8,128)(2,1)}), bf16[4096,512]{1,0:T(8,128)(2,1)}) %all-reduce.9.cloned.1.call-update) | async-done | bytes 4194320 | tf_op jit(solution)/shard_map/psum | solution.py:113
  385.2 6.4 copy.22
  391.6 5.7 all-to-all-start
  397.5 94.5 %all-gather.6.cloned.1.call-done = bf16[8192,256]{1,0:T(8,128)(2,1)} async-done(((bf16[512,256]{1,0:T(8,128)(2,1)}), bf16[8192,256]{1,0:T(8,128)(2,1)}) %all-gather.6.cloned.1.call-update) | async-done | bytes 4194320 | tf_op jit(solution)/shard_map/all_gather | solution.py:120
  492.0 6.5 all-to-all-done
  498.5 4.8 convolution_convert_fusion.1
  504.3 103.7 %all-reduce.11.cloned.1.call-done = f32[256,256]{0,1:T(8,128)} async-done(((f32[256,256]{0,1:T(8,128)}), f32[256,256]{0,1:T(8,128)}) %all-reduce.11.cloned.1.call-update) | async-done | bytes 262160 | tf_op jit(solution)/shard_map/psum | solution.py:125
  608.0 1.1 copy.24
  609.1 1.0 fusion.22
  610.1 11.7 %cholesky.50 = f32[128,128]{1,0:T(8,128)S(1)} custom-call(f32[128,128]{1,0:T(8,128)S(1)} %cholesky.118), custom_call_target="Cholesky" | custom-call | tf_op jit(solution)/shard_map/jit(cholesky)/cholesky | solution.py:126
  621.9 9.8 %custom-call.15 = f32[1,128,128]{1,2,0:T(8,128)S(1)} custom-call(f32[1,128,128]{2,1,0:T(8,128)S(1)} %get-tuple-element.89), custom_call_target="InvertDiagBlocksLowerTriangular" | custom-call | tf_op jit(solution)/shard_map/jit(cholesky)/cholesky | solution.py:126
  632.2 11.7 %cholesky.105 = f32[128,128]{1,0:T(8,128)S(1)} custom-call(f32[128,128]{1,0:T(8,128)S(1)} %convolution_subtract_fusion.1), custom_call_target="Cholesky" | custom-call | tf_op jit(solution)/shard_map/jit(cholesky)/cholesky | solution.py:126
  646.6 5.3 while.1
  647.4 2.0 bitcast_dynamic-update-slice_fusion.2
  649.9 2.0 bitcast_dynamic-update-slice_fusion.2
  651.9 20.5 %custom-call.16 = f32[2,128,128]{1,2,0:T(8,128)S(1)} custom-call(f32[2,128,128]{2,1,0:T(8,128)} %get-tuple-element.11), custom_call_target="InvertDiagBlocksLowerTriangular" | custom-call | tf_op jit(solution)/shard_map/jit(_solve_triangular)/triangular_solve | solution.py:127
  675.0 1.4 multiply_reduce_fusion.29
  678.6 5.0 psum.36
  684.2 4.4 fusion.17
  689.3 26.6 %all-gather.8.cloned.1.call-done = bf16[4096,256]{0,1:T(8,128)(2,1)} async-done(((bf16[256,256]{0,1:T(8,128)(2,1)}), bf16[4096,256]{0,1:T(8,128)(2,1)}) %all-gather.8.cloned.1.call-update) | async-done | bytes 2097168 | tf_op jit(solution)/shard_map/all_gather | solution.py:134
  716.0 4.2 multiply_reduce_fusion
  720.1 31.6 %psum.39 = f32[256]{0:T(256)S(1)} all-reduce(f32[256]{0:T(256)S(1)} %get-tuple-element.125), channel_id=1, replica_groups=mesh['dp'=2,'fsdp'=16] {'fsdp'}, use_global_device_ids=true, to_apply=%region_43.44 | all-reduce | flops 256 | bytes 2048 | tf_op jit(solution)/shard_map/psum | solution.py:137
  (251 shorter events, 30.9 us)
Async XLA Ops:
  7.2 1.1 copy-start
  7.2 82.5 %all-gather.4.cloned.1.call-start = ((), (), s32[]{:S(2)}) async-start(), calls=%async_computation.2 | async-start | bytes 3342336 | tf_op jit(solution)/shard_map/all_gather | solution.py:62
  45.0 112.9 %reduce-scatter.2.cloned.1.call-start = ((), (), s32[]{:S(2)}) async-start(), calls=%async_computation.3 | async-start | bytes 3342336 | tf_op jit(solution)/shard_map/reduce_scatter | solution.py:88
  50.5 0.7 copy-start.17
  50.5 1.8 copy-start.18
  50.5 334.7 %all-reduce.9.cloned.1.call-start = ((), (), s32[]{:S(2)}) async-start(), calls=%async_computation.4 | async-start | bytes 8388608 | tf_op jit(solution)/shard_map/psum | solution.py:113
  157.9 2.4 copy-start.3
  161.4 6.8 collective-permute-start
  168.2 6.7 collective-permute-start.1
  174.9 6.7 collective-permute-start.2
  181.7 6.7 collective-permute-start.3
  188.4 6.7 collective-permute-start.4
  195.1 6.7 collective-permute-start.5
  201.9 6.7 collective-permute-start.6
  208.6 6.7 collective-permute-start.7
  215.4 43.1 %copy-start.5 = (bf16[192,256]{1,0:T(8,128)(2,1)}, bf16[192,256]{1,0:T(8,128)(2,1)S(1)}, u32[]{:S(2)}) copy-start(bf16[192,256]{1,0:T(8,128)(2,1)S(1)} %collective-permute-done.7) | copy-start | bytes 294916
  215.4 6.7 collective-permute-start.8
  222.1 36.4 %copy-start.7 = (bf16[192,256]{1,0:T(8,128)(2,1)}, bf16[192,256]{1,0:T(8,128)(2,1)S(1)}, u32[]{:S(2)}) copy-start(bf16[192,256]{1,0:T(8,128)(2,1)S(1)} %collective-permute-done.8) | copy-start | bytes 294916
  222.1 6.7 collective-permute-start.9
  228.8 0.6 copy-start.9
  229.5 6.7 collective-permute-start.10
  236.2 0.6 copy-start.11
  236.9 6.7 collective-permute-start.11
  243.6 0.6 copy-start.13
  244.2 6.7 collective-permute-start.12
  251.0 0.6 copy-start.15
  251.6 6.8 collective-permute-start.13
  258.5 7.1 collective-permute-start.14
  258.5 16.2 %copy-start.16 = (bf16[192,256]{1,0:T(8,128)(2,1)S(1)}, bf16[192,256]{1,0:T(8,128)(2,1)}, u32[]{:S(2)}) copy-start(bf16[192,256]{1,0:T(8,128)(2,1)} %copy-done.15) | copy-start | bytes 294916
  258.5 16.2 %copy-start.14 = (bf16[192,256]{1,0:T(8,128)(2,1)S(1)}, bf16[192,256]{1,0:T(8,128)(2,1)}, u32[]{:S(2)}) copy-start(bf16[192,256]{1,0:T(8,128)(2,1)} %copy-done.13) | copy-start | bytes 294916
  258.5 16.2 %copy-start.12 = (bf16[192,256]{1,0:T(8,128)(2,1)S(1)}, bf16[192,256]{1,0:T(8,128)(2,1)}, u32[]{:S(2)}) copy-start(bf16[192,256]{1,0:T(8,128)(2,1)} %copy-done.11) | copy-start | bytes 294916
  258.5 16.3 %copy-start.10 = (bf16[192,256]{1,0:T(8,128)(2,1)S(1)}, bf16[192,256]{1,0:T(8,128)(2,1)}, u32[]{:S(2)}) copy-start(bf16[192,256]{1,0:T(8,128)(2,1)} %copy-done.9) | copy-start | bytes 294916
  258.5 16.3 %copy-start.8 = (bf16[192,256]{1,0:T(8,128)(2,1)S(1)}, bf16[192,256]{1,0:T(8,128)(2,1)}, u32[]{:S(2)}) copy-start(bf16[192,256]{1,0:T(8,128)(2,1)} %copy-done.7) | copy-start | bytes 294916
  258.5 16.3 %copy-start.6 = (bf16[192,256]{1,0:T(8,128)(2,1)S(1)}, bf16[192,256]{1,0:T(8,128)(2,1)}, u32[]{:S(2)}) copy-start(bf16[192,256]{1,0:T(8,128)(2,1)} %copy-done.5) | copy-start | bytes 294916
  258.6 18.1 %copy-start.4 = (bf16[1,192,512]{2,1,0:T(8,128)(2,1)S(1)}, bf16[1,192,512]{2,1,0:T(8,128)(2,1)}, u32[]{:S(2)}) copy-start(bf16[1,192,512]{2,1,0:T(8,128)(2,1)} %param.16) | copy-start | bytes 589828
  275.0 1.7 copy-start.1
  280.0 212.0 %all-gather.6.cloned.1.call-start = ((), (), s32[]{:S(2)}) async-start(), calls=%async_computation.5 | async-start | bytes 4456448 | tf_op jit(solution)/shard_map/all_gather | solution.py:120
  391.6 106.9 %all-to-all-start = ((bf16[16,256,512]{1,2,0:T(8,128)(2,1)}), bf16[16,256,512]{1,2,0:T(8,128)(2,1)}, u32[]{:S(2)}, u32[]{:S(2)}) async-start(bf16[16,256,512]{1,2,0:T(8,128)(2,1)} %copy.22), calls=%async_computation.1 | async-start | bytes 8388608 | tf_op jit(solution)/shard_map/all_to_all | solution.py:117
  397.3 210.7 %all-reduce.11.cloned.1.call-start = ((), (), s32[]{:S(2)}) async-start(), calls=%async_computation.6 | async-start | bytes 524288 | tf_op jit(solution)/shard_map/psum | solution.py:125
  504.2 211.7 %all-gather.8.cloned.1.call-start = ((), (), s32[]{:S(2)}) async-start(), calls=%async_computation.7 | async-start | bytes 2228224 | tf_op jit(solution)/shard_map/all_gather | solution.py:134
  684.2 4.4 copy-start.2
Sparse Core Ops, SparseCore 0:
  45.2 44.4 all-gather.3
  93.5 64.4 reduce-scatter.1
  280.1 105.0 all-reduce.8
  387.5 104.4 all-gather.5
  504.3 103.6 all-reduce.10
  674.2 41.6 all-gather.7
